TPU v7x, 32 devices: a whole 2x2x4 slice. The times are simulated.
32 devices in a mesh: groups: 2 (over x), tensor: 8 (over z, y), seq: 2 (over core).
Axes of the slice: x: 2, y: 2, z: 4, core: 2. Of those that a mesh axis runs over, the one named last changes fastest.
Arguments:
- heads_out: bfloat16 [128, 4096], P(('groups', 'seq'), 'tensor'), parts along dimension 0, may hold values from -6 to 6
- stream_in: bfloat16 [128, 8192], P(('groups', 'seq', 'tensor')), parts along dimension 0, may hold values from -40 to 40, as said below
- proj_levels: bfloat16 [4096, 8192], P('tensor'), may hold values from -8 to 7, as said below
- proj_scale: float32 [8192], replicated, may hold values from 0.001703125 to 0.006796875
- norm_gain: float32 [8192], replicated, may hold values from 0.25 to 1.75
- gate_levels: bfloat16 [8192, 14336], P(None, 'tensor'), may hold values from -8 to 7, as said below
- gate_scale: float32 [14336], P('tensor'), may hold values from 0.0012153398 to 0.004861359
- gate_index: int32 [8, 8], P('tensor'), may hold values from 0 to 1791, as said below
- gate_extra: bfloat16 [8192, 64], P(None, 'tensor'), may hold values from -0.29882812 to 0.29882812
- up_levels: bfloat16 [8192, 14336], P(None, 'tensor'), may hold values from -8 to 7, as said below
- up_scale: float32 [14336], P('tensor'), may hold values from 0.0012153398 to 0.004861359
- up_index: int32 [8, 8], P('tensor'), may hold values from 0 to 1791, as said below
- up_extra: bfloat16 [8192, 64], P(None, 'tensor'), may hold values from -0.29882812 to 0.29882812
- down_levels: bfloat16 [14336, 8192], P('tensor'), may hold values from -8 to 7, as said below
- down_scale: float32 [8192], replicated, may hold values from 0.0009020067 to 0.003591323
- down_index: int32 [8, 8], P('tensor'), may hold values from 0 to 8191, as said below
- down_extra: bfloat16 [14336, 8], P('tensor'), may hold values from -0.29882812 to 0.29882812
Outputs:
- stream_out: bfloat16 [128, 8192], P(('groups', 'seq', 'tensor')), parts along dimension 0
There are 2 independent parts, one for each index of `groups`. A program takes and returns all parts, laid end to end along the dimension named above; an argument that names none is the same for every part. Nothing has to cross between parts.
Inputs may be any that keep to these rules, and one draw needn't show every extreme that they name: stream_in has rows and columns of differing scales. `proj_levels`: integer values. `gate_levels`: integer values. `up_levels`: integer values. `down_levels`: integer values. `gate_index`: each row holds 8 different numbers. `up_index`: each row holds 8 different numbers. `down_index`: each row holds 8 different numbers.
All inputs are finite; a program needn't handle non-finite values.
Results may differ from a plain program's by a relative error of at most 0.0055.
Values may be sent and summed in bfloat16 or wider, within the bound.
No kernel may reach another device: no remote copies, remote signals or barrier semaphores. Data moves between devices by JAX's collectives and lax.ppermute only.
A program may use at most 192 MiB of HBM per device.

v0:
```python
import jax
import jax.numpy as jnp
from jax import lax
from jax.sharding import PartitionSpec as P


def rms_norm(mixed, norm_gain):
    mean_sq = jnp.mean(mixed * mixed, axis=-1, keepdims=True)
    return (mixed * lax.rsqrt(mean_sq + 1e-05) * norm_gain).astype(jnp.bfloat16)


def picker(index_row, width):
    return (index_row[:, None] == jnp.arange(width, dtype=jnp.int32)[None, :]).astype(jnp.float32)


def project(rows_in, levels, scale, extra, chosen):
    base = jnp.dot(rows_in, levels, preferred_element_type=jnp.float32)
    added = jnp.dot(rows_in, extra, preferred_element_type=jnp.float32)
    return base * scale + jnp.dot(added, chosen, precision=lax.Precision.HIGHEST)


def local(
    heads_out,
    stream_in,
    proj_levels,
    proj_scale,
    norm_gain,
    gate_levels,
    gate_scale,
    gate_index,
    gate_extra,
    up_levels,
    up_scale,
    up_index,
    up_extra,
    down_levels,
    down_scale,
    down_index,
    down_extra,
):
    own_rows = stream_in.shape[0]
    shard_width = gate_levels.shape[1]
    model_width = proj_levels.shape[1]
    gate_pick = picker(gate_index[0], shard_width)
    up_pick = picker(up_index[0], shard_width)
    down_pick = picker(down_index[0], model_width)
    total = lax.psum(
        jnp.dot(heads_out, proj_levels, preferred_element_type=jnp.float32) * proj_scale, "tensor"
    )
    stream_all = lax.all_gather(stream_in, "tensor", axis=0, tiled=True)
    mixed_all = stream_all.astype(jnp.float32) + total
    normed_rows = rms_norm(mixed_all, norm_gain)
    gate = project(normed_rows, gate_levels, gate_scale, gate_extra, gate_pick)
    up = project(normed_rows, up_levels, up_scale, up_extra, up_pick)
    hidden = (jax.nn.silu(gate) * up).astype(jnp.bfloat16)
    mixed = lax.dynamic_slice_in_dim(mixed_all, lax.axis_index("tensor") * own_rows, own_rows, 0)
    down = lax.psum_scatter(
        project(hidden, down_levels, down_scale, down_extra, down_pick),
        "tensor",
        scatter_dimension=0,
        tiled=True,
    )
    return (mixed + down).astype(jnp.bfloat16)


def solution(mesh):
    placed = (
        P(("groups", "seq"), "tensor"),
        P(("groups", "seq", "tensor"), None),
        P("tensor", None),
        P(),
        P(),
        P(None, "tensor"),
        P("tensor"),
        P("tensor", None),
        P(None, "tensor"),
        P(None, "tensor"),
        P("tensor"),
        P("tensor", None),
        P(None, "tensor"),
        P("tensor", None),
        P(),
        P("tensor", None),
        P("tensor", None),
    )
    return jax.shard_map(
        local,
        mesh=mesh,
        in_specs=placed,
        out_specs=P(("groups", "seq", "tensor"), None),
        check_vma=False,
    )
```

profile of v0, /device:TPU:0, one launch (start us, length us, event | category | flops | bytes accessed | tf_op | source)
XLA Modules:
  0.0 225.5 jit_solution(14587140887796130153)
XLA Ops:
  6.5 6.0 %convolution_multiply_fusion.1 = f32[32,8192]{1,0:T(8,128)} fusion(bf16[32,512]{1,0:T(8,128)(2,1)} %param.17, bf16[512,8192]{1,0:T(8,128)(2,1)} %param.19, f32[8192]{0:T(1024)} %param.20), kind=kOutput, calls=%fused_computation.2 | convolution fusion | flops 268697600 | bytes 9502720 | tf_op jit(solution)/shard_map/dot_general | solution.py:48
  12.5 0.0 all-reduce.4.cloned.1.call-update
  12.6 0.0 all-reduce.6.cloned.1.call-start
  12.6 35.1 %all-gather = bf16[8,4,8192]{2,1,0:T(4,128)(2,1)S(1)} all-gather(bf16[1,4,8192]{2,1,0:T(4,128)(2,1)} %bitcast.22), channel_id=1, replica_groups=mesh['groups'=2,'tensor'=8,'seq'=2] {'tensor'}, dimensions={0}, use_global_device_ids=true | all-gather | bytes 589824 | tf_op jit(solution)/shard_map/all_gather | solution.py:50
  47.7 0.1 reshape.18
  47.8 48.7 %all-reduce.4.cloned.1.call-done = f32[32,8192]{1,0:T(8,128)} async-done(((f32[32,8192]{1,0:T(8,128)}), f32[32,8192]{1,0:T(8,128)}) %all-reduce.4.cloned.1.call-update) | async-done | bytes 1048592 | tf_op jit(solution)/shard_map/psum | solution.py:47
  96.4 1.4 multiply_reduce_fusion
  97.9 0.9 multiply_convert_fusion
  98.8 0.3 fusion.6
  99.1 1.2 fusion.7
  100.3 0.0 copy-start.5
  100.4 12.0 %convolution_multiply_fusion.3 = f32[32,1792]{1,0:T(8,128)S(1)} fusion(bf16[32,8192]{1,0:T(8,128)(2,1)S(1)} %multiply_convert_fusion, bf16[8192,1792]{1,0:T(8,128)(2,1)} %param.22, f32[1792]{0:T(1024)} %param.23), kind=kOutput, calls=%fused_computation.7 | convolution fusion | flops 939581440 | bytes 30120960 | tf_op jit(solution)/shard_map/dot_general | solution.py:17
  112.4 0.0 copy-start.8
  112.4 12.0 %convolution_multiply_fusion.2 = f32[32,1792]{1,0:T(8,128)S(1)} fusion(bf16[32,8192]{1,0:T(8,128)(2,1)S(1)} %multiply_convert_fusion, bf16[8192,1792]{1,0:T(8,128)(2,1)} %param.26, f32[1792]{0:T(1024)S(1)} %copy-done.4), kind=kOutput, calls=%fused_computation.5 | convolution fusion | flops 939581440 | bytes 30120960 | tf_op jit(solution)/shard_map/dot_general | solution.py:17
  124.4 0.3 convolution_add_fusion.2
  124.7 0.3 fusion.1
  125.1 0.1 fusion.8
  125.2 0.0 copy-done.2
  125.2 12.0 %convolution_multiply_fusion = f32[32,8192]{1,0:T(8,128)S(1)} fusion(bf16[32,1792]{1,0:T(8,128)(2,1)S(1)} %fusion.1, bf16[1792,8192]{1,0:T(8,128)(2,1)} %param.30, f32[8192]{0:T(1024)S(1)} %copy-done.2), kind=kOutput, calls=%fused_computation.1 | convolution fusion | flops 939786240 | bytes 30556160 | tf_op jit(solution)/shard_map/dot_general | solution.py:17
  137.2 1.7 convolution_add_fusion
  138.9 0.0 all-reduce.6.cloned.1.call-update
  139.0 0.6 dynamic-slice
  140.2 76.8 %all-reduce.6.cloned.1.call-done = f32[32,8192]{1,0:T(8,128)} async-done(((f32[32,8192]{1,0:T(8,128)}), f32[32,8192]{1,0:T(8,128)}) %all-reduce.6.cloned.1.call-update) | async-done | bytes 1048592
  217.0 1.6 fusion.2
  (17 shorter events, 0.1 us)
Async XLA Ops:
  6.5 92.3 %copy-start = (bf16[8192,8]{0,1:T(8,128)(2,1)S(1)}, bf16[8192,8]{0,1:T(8,128)(2,1)}, u32[]{:S(2)}) copy-start(bf16[8192,8]{0,1:T(8,128)(2,1)} %param.25) | copy-start | bytes 393220
  6.5 105.8 %copy-start.4 = (f32[1792]{0:T(1024)S(1)}, f32[1792]{0:T(1024)}, u32[]{:S(2)}) copy-start(f32[1792]{0:T(1024)} %param.27) | copy-start | bytes 21508
  6.5 89.9 %all-reduce.4.cloned.1.call-start = ((), (), s32[]{:S(2)}) async-start(), calls=%async_computation | async-start | bytes 2097152 | tf_op jit(solution)/shard_map/psum | solution.py:47
  12.6 204.5 %all-reduce.6.cloned.1.call-start = ((), (), s32[]{:S(2)}) async-start(), calls=%async_computation.1 | async-start | bytes 2097152
  100.3 24.1 %copy-start.5 = (s32[1,8]{1,0:T(1,128)S(1)}, s32[1,8]{1,0:T(1,128)}, u32[]{:S(2)}) copy-start(s32[1,8]{1,0:T(1,128)} %param.24) | copy-start | bytes 100
  100.3 24.4 %copy-start.7 = (s32[1,8]{1,0:T(1,128)S(1)}, s32[1,8]{1,0:T(1,128)}, u32[]{:S(2)}) copy-start(s32[1,8]{1,0:T(1,128)} %param.28) | copy-start | bytes 100
  100.3 24.7 %copy-start.3 = (bf16[1792,8]{0,1:T(8,128)(2,1)S(1)}, bf16[1792,8]{0,1:T(8,128)(2,1)}, u32[]{:S(2)}) copy-start(bf16[1792,8]{0,1:T(8,128)(2,1)} %param.33) | copy-start | bytes 86020
  100.4 24.8 %copy-start.2 = (f32[8192]{0:T(1024)S(1)}, f32[8192]{0:T(1024)}, u32[]{:S(2)}) copy-start(f32[8192]{0:T(1024)} %param.31) | copy-start | bytes 98308
  112.4 24.9 %copy-start.6 = (s32[1,8]{1,0:T(1,128)S(1)}, s32[1,8]{1,0:T(1,128)}, u32[]{:S(2)}) copy-start(s32[1,8]{1,0:T(1,128)} %param.32) | copy-start | bytes 100
  112.4 26.6 %copy-start.8 = (u32[32]{0:T(128)S(1)}, u32[32]{0:T(128)}, u32[]{:S(2)}) copy-start(u32[32]{0:T(128)} %constant.28) | copy-start | bytes 388
  112.4 106.3 %copy-start.1 = (bf16[8192,8]{0,1:T(8,128)(2,1)S(1)}, bf16[8192,8]{0,1:T(8,128)(2,1)}, u32[]{:S(2)}) copy-start(bf16[8192,8]{0,1:T(8,128)(2,1)} %param.25) | copy-start | bytes 393220
Sparse Core Ops, SparseCore 0:
  12.7 83.7 all-reduce.3
  139.1 77.9 all-reduce.5
where the time goes:
time: 226 us
  waiting for transfers between devices  126 us (56%)
  matrix products  45.9 us (20%)
  blocking collectives  35.1 us (16%)
  between operations  14.2 us (6%)
  other arithmetic  4.02 us (2%)
    unnamed x3, waiting for transfers between devices  76.9 us
    psum x1, waiting for transfers between devices, local(): lax.psum(jnp.dot(heads_out, proj_levels, preferred_element_type=jnp.float...  48.7 us
    dot_general x3, matrix products, project(): base = jnp.dot(rows_in, levels, preferred_element_type=jnp.float32)  36 us
    all_gather x1, blocking collectives, local(): stream_all = lax.all_gather(stream_in, 'tensor', axis=0, tiled=True)  35.1 us
    dot_general x1, matrix products, local(): jnp.dot(heads_out, proj_levels, preferred_element_type=jnp.float32)  6 us
  transfers between devices with their start and end apart: 2, of which 2 were waited for; matrix products, arithmetic and copies ran while one was open for 0% of the time, Pallas kernels for 0%

commit v1 on v0

--- a/solution.py
+++ b/solution.py
@@ -1,7 +1,17 @@
+import functools
 import jax
 import jax.numpy as jnp
 from jax import lax
 from jax.sharding import PartitionSpec as P
+
+
+def tokens_run(local_array, axis_key):
+    y_new = lax.all_gather(local_array, axis_key)
+    part_now = jnp.sum(y_new, axis=0)
+    return part_now
+
+
+_wrap_column = functools.partial(tokens_run, axis_key="tensor")
 
 
 def rms_norm(mixed, norm_gain):
@@ -44,8 +54,8 @@
     gate_pick = picker(gate_index[0], shard_width)
     up_pick = picker(up_index[0], shard_width)
     down_pick = picker(down_index[0], model_width)
-    total = lax.psum(
-        jnp.dot(heads_out, proj_levels, preferred_element_type=jnp.float32) * proj_scale, "tensor"
+    total = _wrap_column(
+        jnp.dot(heads_out, proj_levels, preferred_element_type=jnp.float32) * proj_scale
     )
     stream_all = lax.all_gather(stream_in, "tensor", axis=0, tiled=True)
     mixed_all = stream_all.astype(jnp.float32) + total

time: 226 us -> 272 us (1.20)
  waiting for transfers between devices: 126 us -> 170 us
    all_gather x0 -> x1, waiting for transfers between devices: none -> 94.7 us  [tokens_run(): y_new = lax.all_gather(local_array, axis_key)]
    psum x1 -> x0, waiting for transfers between devices: 48.7 us -> none  [local(): lax.psum(jnp.dot(heads_out, proj_levels, preferred_element_type=jnp.float...]
    reduce_sum x0 -> x1, other arithmetic: none -> 3.91 us  [tokens_run(): part_now = jnp.sum(y_new, axis=0)]
where the time goes in v1:
time: 272 us
  waiting for transfers between devices  170 us (62%)
  matrix products  45 us (17%)
  blocking collectives  35.5 us (13%)
  between operations  14.3 us (5%)
  other arithmetic  5.94 us (2%)
    all_gather x1, waiting for transfers between devices, tokens_run(): y_new = lax.all_gather(local_array, axis_key)  94.7 us
    unnamed x3, waiting for transfers between devices  75.4 us
    dot_general x3, matrix products, project(): base = jnp.dot(rows_in, levels, preferred_element_type=jnp.float32)  36 us
    all_gather x1, blocking collectives, local(): stream_all = lax.all_gather(stream_in, 'tensor', axis=0, tiled=True)  35.5 us
    dot_general x1, matrix products, local(): jnp.dot(heads_out, proj_levels, preferred_element_type=jnp.float32)  6.07 us
  transfers between devices with their start and end apart: 2, of which 2 were waited for; matrix products, arithmetic and copies ran while one was open for 0% of the time, Pallas kernels for 0%

profile of v1, /device:TPU:0, one launch (start us, length us, event | category | flops | bytes accessed | tf_op | source)
XLA Modules:
  0.0 271.6 jit_solution(10732890700718917495)
XLA Ops:
  6.5 0.0 all-gather.4.cloned.1.call-start
  6.6 6.1 %convolution_multiply_fusion.1 = f32[32,8192]{1,0:T(8,128)} fusion(bf16[32,512]{1,0:T(8,128)(2,1)} %param.17, bf16[512,8192]{1,0:T(8,128)(2,1)} %param.19, f32[8192]{0:T(1024)} %param.20), kind=kOutput, calls=%fused_computation.2 | convolution fusion | flops 268697600 | bytes 9502720 | tf_op jit(solution)/shard_map/dot_general | solution.py:58
  12.7 0.0 all-gather.4.cloned.1.call-update
  12.7 0.0 all-reduce.3.cloned.1.call-start
  12.7 35.5 %all-gather.1 = bf16[8,4,8192]{2,1,0:T(4,128)(2,1)S(1)} all-gather(bf16[1,4,8192]{2,1,0:T(4,128)(2,1)} %bitcast.24), channel_id=1, replica_groups=mesh['groups'=2,'tensor'=8,'seq'=2] {'tensor'}, dimensions={0}, use_global_device_ids=true | all-gather | bytes 589824 | tf_op jit(solution)/shard_map/all_gather | solution.py:60
  48.2 0.1 reshape.19
  48.3 94.7 %all-gather.4.cloned.1.call-done = f32[256,8192]{1,0:T(8,128)} async-done(((f32[32,8192]{1,0:T(8,128)}), f32[256,8192]{1,0:T(8,128)}) %all-gather.4.cloned.1.call-update) | async-done | bytes 8388624 | tf_op jit(solution)/shard_map/all_gather | solution.py:9
  143.1 3.9 %reduce_sum.18 = f32[32,8192]{1,0:T(8,128)S(1)} reduce(f32[8,32,8192]{2,1,0:T(8,128)} %bitcast.23, f32[]{:T(128)} %constant.4.clone.1), dimensions={0}, to_apply=%region_0.0 | reduce | flops 1835008 | bytes 9437188 | tf_op jit(solution)/shard_map/reduce_sum | solution.py:10
  147.0 0.2 multiply_reduce_fusion
  147.2 0.2 multiply_convert_fusion
  147.4 0.3 fusion.6
  147.7 0.0 copy-done.9
  147.7 0.3 fusion.7
  148.0 12.0 %convolution_multiply_fusion.3 = f32[32,1792]{1,0:T(8,128)S(1)} fusion(bf16[32,8192]{1,0:T(8,128)(2,1)S(1)} %multiply_convert_fusion, bf16[8192,1792]{1,0:T(8,128)(2,1)} %param.22, f32[1792]{0:T(1024)S(1)} %copy-done.5), kind=kOutput, calls=%fused_computation.7 | convolution fusion | flops 939581440 | bytes 30120960 | tf_op jit(solution)/shard_map/dot_general | solution.py:27
  160.0 12.0 %convolution_multiply_fusion.2 = f32[32,1792]{1,0:T(8,128)S(1)} fusion(bf16[32,8192]{1,0:T(8,128)(2,1)S(1)} %multiply_convert_fusion, bf16[8192,1792]{1,0:T(8,128)(2,1)} %param.26, f32[1792]{0:T(1024)S(1)} %copy-done.6), kind=kOutput, calls=%fused_computation.5 | convolution fusion | flops 939581440 | bytes 30120960 | tf_op jit(solution)/shard_map/dot_general | solution.py:27
  172.1 0.3 convolution_add_fusion.2
  172.4 0.3 fusion.1
  172.7 0.1 fusion.8
  172.8 0.0 copy-done.2
  172.8 12.0 %convolution_multiply_fusion = f32[32,8192]{1,0:T(8,128)S(1)} fusion(bf16[32,1792]{1,0:T(8,128)(2,1)S(1)} %fusion.1, bf16[1792,8192]{1,0:T(8,128)(2,1)} %param.30, f32[8192]{0:T(1024)S(1)} %copy-done.2), kind=kOutput, calls=%fused_computation.1 | convolution fusion | flops 939786240 | bytes 30556160 | tf_op jit(solution)/shard_map/dot_general | solution.py:27
  184.9 1.6 convolution_add_fusion
  186.6 0.6 dynamic-slice
  187.8 75.3 %all-reduce.3.cloned.1.call-done = f32[32,8192]{1,0:T(8,128)} async-done(((f32[32,8192]{1,0:T(8,128)}), f32[32,8192]{1,0:T(8,128)}) %all-reduce.3.cloned.1.call-update) | async-done | bytes 1048592
  263.2 1.6 fusion.2
  (24 shorter events, 0.1 us)
Async XLA Ops:
  6.5 140.8 %copy-start = (bf16[8192,8]{0,1:T(8,128)(2,1)S(1)}, bf16[8192,8]{0,1:T(8,128)(2,1)}, u32[]{:S(2)}) copy-start(bf16[8192,8]{0,1:T(8,128)(2,1)} %param.25) | copy-start | bytes 393220
  6.5 140.7 %copy-start.3 = (f32[8192]{0:T(1024)S(1)}, f32[8192]{0:T(1024)}, u32[]{:S(2)}) copy-start(f32[8192]{0:T(1024)} %param.21) | copy-start | bytes 98308
  6.5 141.1 %copy-start.9 = (bf16[8192,8]{0,1:T(8,128)(2,1)S(1)}, bf16[8192,8]{0,1:T(8,128)(2,1)}, u32[]{:S(2)}) copy-start(bf16[8192,8]{0,1:T(8,128)(2,1)} %param.29) | copy-start | bytes 393220
  6.5 141.4 %copy-start.5 = (f32[1792]{0:T(1024)S(1)}, f32[1792]{0:T(1024)}, u32[]{:S(2)}) copy-start(f32[1792]{0:T(1024)} %param.23) | copy-start | bytes 21508
  6.5 136.5 %all-gather.4.cloned.1.call-start = ((), (), s32[]{:S(2)}) async-start(), calls=%async_computation | async-start | bytes 9437184 | tf_op jit(solution)/shard_map/all_gather | solution.py:9
  12.7 147.3 %copy-start.6 = (f32[1792]{0:T(1024)S(1)}, f32[1792]{0:T(1024)}, u32[]{:S(2)}) copy-start(f32[1792]{0:T(1024)} %param.27) | copy-start | bytes 21508
  12.7 250.5 %all-reduce.3.cloned.1.call-start = ((), (), s32[]{:S(2)}) async-start(), calls=%async_computation.1 | async-start | bytes 2097152
  148.0 24.1 %copy-start.7 = (s32[1,8]{1,0:T(1,128)S(1)}, s32[1,8]{1,0:T(1,128)}, u32[]{:S(2)}) copy-start(s32[1,8]{1,0:T(1,128)} %param.24) | copy-start | bytes 100
  148.0 24.4 %copy-start.10 = (s32[1,8]{1,0:T(1,128)S(1)}, s32[1,8]{1,0:T(1,128)}, u32[]{:S(2)}) copy-start(s32[1,8]{1,0:T(1,128)} %param.28) | copy-start | bytes 100
  148.0 24.7 %copy-start.4 = (bf16[1792,8]{0,1:T(8,128)(2,1)S(1)}, bf16[1792,8]{0,1:T(8,128)(2,1)}, u32[]{:S(2)}) copy-start(bf16[1792,8]{0,1:T(8,128)(2,1)} %param.33) | copy-start | bytes 86020
  148.0 24.8 %copy-start.2 = (f32[8192]{0:T(1024)S(1)}, f32[8192]{0:T(1024)}, u32[]{:S(2)}) copy-start(f32[8192]{0:T(1024)} %param.31) | copy-start | bytes 98308
  160.0 24.9 %copy-start.8 = (s32[1,8]{1,0:T(1,128)S(1)}, s32[1,8]{1,0:T(1,128)}, u32[]{:S(2)}) copy-start(s32[1,8]{1,0:T(1,128)} %param.32) | copy-start | bytes 100
  160.0 26.5 %copy-start.11 = (u32[32]{0:T(128)S(1)}, u32[32]{0:T(128)}, u32[]{:S(2)}) copy-start(u32[32]{0:T(128)} %constant.28) | copy-start | bytes 388
  160.0 104.8 %copy-start.1 = (bf16[8192,8]{0,1:T(8,128)(2,1)S(1)}, bf16[8192,8]{0,1:T(8,128)(2,1)}, u32[]{:S(2)}) copy-start(bf16[8192,8]{0,1:T(8,128)(2,1)} %param.25) | copy-start | bytes 393220
Sparse Core Ops, SparseCore 0:
  12.8 130.2 all-gather.3
  186.7 76.4 all-reduce.2
